TPU v7x, 1024 devices: a whole 4x4x32 slice. The times are simulated.
1024 devices in a mesh: seq: 16 (over y, x), frame: 64 (over z, core).
Axes of the slice: x: 4, y: 4, z: 32, core: 2. Of those that a mesh axis runs over, the one named last changes fastest.
Arguments:
- value_grad: bfloat16 [64, 16384, 512], P('frame', 'seq'), may hold values from -6 to 6
- w_value: bfloat16 [8192, 512], P('seq'), may hold values from -0.25 to 0.25
- norm_gain: float32 [8192], P('seq'), may hold values from 0.1 to 1.9
- vis_pos: int32 [64, 128], P('frame'), may hold values from 0 to 16383, as said below
- frame_owner: int32 [64, 128, 1], P('frame'), may hold values from 0 to 63; in each aligned block of 128 rows (0 to 127, 128 to 255, ..., all dimensions but the last counted through in order) at most 4 rows name the same one
- ques_span: int32 [64, 2], P('frame'), may hold values from 0 to 32, as said below
- vis_proj: bfloat16 [64, 128, 8192], P('frame', None, 'seq')
- vis_resid: bfloat16 [64, 128, 8192], P('frame', None, 'seq'), may hold values from -6 to 6
- ques_hidden: bfloat16 [64, 32, 8192], P('frame', None, 'seq'), may hold values from -6 to 6
- w_down: bfloat16 [8192, 8192], P(None, 'seq'), may hold values from -0.0625 to 0.0625
- pre_owned: bfloat16 [64, 8192, 256], P('frame', 'seq'), may hold values from -6 to 6
Outputs:
- pre_grad: bfloat16 [64, 8192, 256], P('frame', 'seq')
- ques_grad: bfloat16 [64, 32, 8192], P('frame', None, 'seq')
Inputs may be any that keep to these rules, and one draw needn't show every extreme that they name: `vis_pos`: each row is distinct and increasing. `frame_owner`: in each sequence at most 4 visual tokens name the same owner. `ques_span`: column 1 is at least 1, and column 0 plus column 1 is at most 32.
All inputs are finite; a program needn't handle non-finite values.
Results may differ from a plain program's by a relative error of at most 0.015.
Values may be sent and summed in bfloat16 or wider, within the bound.
A program may use at most 64 MiB of HBM per device.

v0:
```python
import math

import jax
import jax.numpy as jnp
from jax import lax
from jax.sharding import PartitionSpec as P

D = 8192


epsilon = 1e-06


def gelu_slope(pre_act):
    normal_cdf = 0.5 * (1.0 + lax.erf(pre_act * 0.7071067811865476))
    density = jnp.exp(-0.5 * pre_act * pre_act) * 0.3989422804014327
    return normal_cdf + pre_act * density


def body(
    value_grad,
    w_value,
    norm_gain,
    vis_pos,
    frame_owner,
    ques_span,
    vis_proj,
    vis_resid,
    ques_hidden,
    w_down,
    pre_owned,
):
    positions = vis_pos[0]
    local_rows = value_grad[0]
    shard_len = local_rows.shape[0]
    projected = vis_proj[0].astype(jnp.float32)
    residual = vis_resid[0].astype(jnp.float32)
    span_start = ques_span[0, 0]
    span_count = ques_span[0, 1]
    places = jnp.arange(ques_hidden.shape[1], dtype=jnp.int32)
    span_mask = ((places >= span_start) & (places < span_start + span_count)).astype(jnp.float32)
    count_value = span_count.astype(jnp.float32)
    quest_mean = (
        jnp.dot(
            span_mask.astype(jnp.bfloat16)[None, :],
            ques_hidden[0],
            preferred_element_type=jnp.float32,
        )[0]
        / count_value
    )
    sum_query = jnp.sum(projected * quest_mean[None, :], axis=1)
    sum_square = jnp.sum(projected * projected, axis=1)
    sum_query, sum_square = lax.psum((sum_query, sum_square), "seq")
    offset = lax.axis_index("seq") * shard_len
    token_index = offset + jnp.arange(shard_len, dtype=jnp.int32)
    select = (positions[:, None] == token_index[None, :]).astype(jnp.bfloat16)
    own_rows = jnp.dot(select, local_rows, preferred_element_type=jnp.float32)
    picked = lax.psum(own_rows.astype(jnp.bfloat16), "seq")
    normed_grad = jnp.einsum("jk,dk->jd", picked, w_value, preferred_element_type=jnp.float32)
    sum_norm = jnp.sum(norm_gain[None, :] * normed_grad * projected, axis=1)
    sum_resid = jnp.sum(residual * projected, axis=1)
    sum_norm, sum_resid = lax.psum((sum_norm, sum_resid), "seq")
    gate_scale = 4.0 / math.sqrt(D)
    gate_value = jax.nn.sigmoid(gate_scale * sum_query)
    inv_rms = lax.rsqrt(gate_value * gate_value * sum_square / D + epsilon)
    inner_sum = gate_value * sum_norm
    coef_value = gate_value * inv_rms * inv_rms * inv_rms * inner_sum / D
    input_grad = (
        residual
        + inv_rms[:, None] * norm_gain[None, :] * normed_grad
        - coef_value[:, None] * projected
    )
    gate_grad = sum_resid + inv_rms * sum_norm - coef_value * sum_square
    logit_grad = gate_grad * gate_value * (1.0 - gate_value)
    proj_grad = (
        gate_value[:, None] * input_grad + (logit_grad * gate_scale)[:, None] * quest_mean[None, :]
    ).astype(jnp.bfloat16)
    quest_grad = jnp.sum((logit_grad * gate_scale)[:, None] * projected, axis=0)
    ques_out = (span_mask[:, None] * quest_grad[None, :] / count_value).astype(jnp.bfloat16)[None]
    owners_count = lax.axis_size("frame")
    slot_total = pre_owned.shape[2]
    capacity = slot_total // owners_count
    owners = frame_owner[0, :, 0]
    owner_hot = (owners[:, None] == jnp.arange(owners_count, dtype=jnp.int32)[None, :]).astype(
        jnp.int32
    )
    earlier = jnp.cumsum(owner_hot, axis=0) - owner_hot
    rank_in_owner = jnp.sum(earlier * owner_hot, axis=1)
    targets = owners * capacity + rank_in_owner
    placing = (jnp.arange(slot_total, dtype=jnp.int32)[:, None] == targets[None, :]).astype(
        jnp.bfloat16
    )
    outgoing = jnp.dot(placing, proj_grad, preferred_element_type=jnp.float32).astype(jnp.bfloat16)
    incoming = lax.all_to_all(outgoing, "frame", split_axis=0, concat_axis=0, tiled=True)
    hidden_sum = lax.psum_scatter(
        jnp.einsum("hd,nd->hn", w_down, incoming, preferred_element_type=jnp.float32).astype(
            jnp.bfloat16
        ),
        "seq",
        scatter_dimension=0,
        tiled=True,
    ).astype(jnp.float32)
    pre_act = pre_owned[0].astype(jnp.float32)
    pre_out = (hidden_sum * gelu_slope(pre_act)).astype(jnp.bfloat16)[None]
    return (pre_out, ques_out)


def solution(mesh):
    in_specs = (
        P("frame", "seq", None),
        P("seq", None),
        P("seq"),
        P("frame", None),
        P("frame", None, None),
        P("frame", None),
        P("frame", None, "seq"),
        P("frame", None, "seq"),
        P("frame", None, "seq"),
        P(None, "seq"),
        P("frame", "seq", None),
    )
    out_specs = (P("frame", "seq", None), P("frame", None, "seq"))
    return jax.shard_map(body, mesh=mesh, in_specs=in_specs, out_specs=out_specs, check_vma=False)
```

profile of v0, /device:TPU:1, one launch (start us, length us, event | category | flops | bytes accessed | tf_op | source)
XLA Modules:
  0.0 388.4 jit_solution(10475802596974169158)
XLA Ops:
  7.2 0.0 copy-start
  7.2 0.0 all-reduce.3.cloned.1.call-start
  7.2 1.2 copy-done
  8.4 1.7 convolution_convert_fusion.2
  10.1 0.0 all-reduce.3.cloned.1.call-update
  10.1 0.0 reduce-scatter.2.cloned.1.call-start
  10.1 1.3 fusion.40
  13.3 0.6 and_convert_fusion
  13.9 0.7 fusion.33
  14.6 0.2 reduce_window_sum.11
  14.8 0.8 select_reduce_fusion
  15.6 0.9 fusion.34
  16.5 0.7 multiply_add_fusion
  17.2 156.1 %all-reduce.3.cloned.1.call-done = bf16[128,512]{1,0:T(8,128)(2,1)} async-done(((bf16[128,512]{1,0:T(8,128)(2,1)}), bf16[128,512]{1,0:T(8,128)(2,1)}) %all-reduce.3.cloned.1.call-update) | async-done | bytes 131088 | tf_op jit(solution)/shard_map/psum | solution.py:58
  173.3 1.6 fusion.17
  174.9 31.0 %all-reduce = (f32[128]{0:T(128)S(1)}, f32[128]{0:T(128)S(1)}, f32[128]{0:T(128)S(1)}, f32[128]{0:T(128)S(1)}) all-reduce(f32[128]{0:T(128)S(1)} %get-tuple-element.7, f32[128]{0:T(128)S(1)} %get-tuple-element.6, f32[128]{0:T(128)S(1)} %get-tuple-element.5, f32[128]{0:T(128)S(1)} %get-tuple-element.4), channel_id=1, replica_groups=mesh['seq'=16,'frame'=64] {'seq'}, use_global_device_ids=true, to_apply=%region_3.0 | all-reduce | flops 512 | bytes 4096 | tf_op jit(solution)/shard_map/psum | solution.py:53
  206.0 1.3 convolution_convert_fusion.1
  207.3 0.1 all_to_all.8
  207.4 73.8 %all_to_all.12 = bf16[64,4,512]{2,1,0:T(4,128)(2,1)S(1)} all-to-all(bf16[64,4,512]{2,1,0:T(4,128)(2,1)S(1)} %all_to_all.8), channel_id=1, replica_groups=mesh['seq'=16,'frame'=64] {'frame'}, dimensions={0} | all-to-all | bytes 524288 | tf_op jit(solution)/shard_map/all_to_all | solution.py:94
  281.1 0.1 all_to_all.10
  281.2 0.0 copy-start.2
  281.2 0.0 copy-start.1
  281.2 7.9 %fusion = bf16[8192,256]{0,1:T(8,128)(2,1)} fusion(bf16[256,512]{1,0:T(8,128)(2,1)S(1)} %all_to_all.10, bf16[8192,512]{1,0:T(8,128)(2,1)} %param.20), kind=kOutput, calls=%fused_computation.1 | convolution fusion | flops 2149580800 | bytes 12845056 | tf_op jit(solution)/shard_map/hd,nd->hn/dot_general | solution.py:96
  289.2 0.0 reduce-scatter.2.cloned.1.call-update
  289.2 0.0 copy-done.2
  289.2 0.1 copy.13
  289.4 0.0 copy-done.1
  289.4 0.1 fusion.19
  289.5 0.7 divide_convert_fusion
  290.2 89.3 %reduce-scatter.2.cloned.1.call-done = bf16[512,256]{0,1:T(8,128)(2,1)} async-done(((bf16[8192,256]{0,1:T(8,128)(2,1)}), bf16[512,256]{0,1:T(8,128)(2,1)}) %reduce-scatter.2.cloned.1.call-update) | async-done | bytes 262160 | tf_op jit(solution)/shard_map/reduce_scatter | solution.py:95
  379.5 1.2 fusion.22
  380.7 0.8 copy.14
  (4 shorter events, 0.0 us)
Async XLA Ops:
  7.2 1.2 copy-start
  7.2 166.1 %all-reduce.3.cloned.1.call-start = ((), (), s32[]{:S(2)}) async-start(), calls=%async_computation.2 | async-start | bytes 262144 | tf_op jit(solution)/shard_map/psum | solution.py:58
  10.1 369.4 %reduce-scatter.2.cloned.1.call-start = ((), (), s32[]{:S(2)}) async-start(), calls=%async_computation.3 | async-start | bytes 4456448 | tf_op jit(solution)/shard_map/reduce_scatter | solution.py:95
  281.2 8.0 %copy-start.2 = (bf16[1,512,256]{2,1,0:T(8,128)(2,1)S(1)}, bf16[1,512,256]{2,1,0:T(8,128)(2,1)}, u32[]{:S(2)}) copy-start(bf16[1,512,256]{2,1,0:T(8,128)(2,1)} %param.21) | copy-start | bytes 786436
  281.2 8.1 %copy-start.1 = (bf16[1,128,512]{2,1,0:T(8,128)(2,1)S(1)}, bf16[1,128,512]{2,1,0:T(8,128)(2,1)}, u32[]{:S(2)}) copy-start(bf16[1,128,512]{2,1,0:T(8,128)(2,1)} %param.17) | copy-start | bytes 393220
Sparse Core Ops, SparseCore 0:
  11.8 161.4 all-reduce.2
  289.3 90.1 reduce-scatter.1
where the time goes:
time: 390 us; the launch traced here: 388 us
  waiting for transfers between devices  245 us (63%)
  blocking collectives  105 us (27%)
  between operations  16 us (4%)
  matrix products  13.4 us (3%)
  other arithmetic  5.01 us (1%)
    psum x1, waiting for transfers between devices, body(): picked = lax.psum(own_rows.astype(jnp.bfloat16), 'seq')  156 us
    reduce_scatter x1, waiting for transfers between devices, body(): lax.psum_scatter(jnp.einsum('hd,nd->hn', w_down, incoming, preferred_elem...  89.3 us
    all_to_all x1, blocking collectives, body(): lax.all_to_all(outgoing, 'frame', split_axis=0, concat_axis=0, tiled=True)  73.8 us
    psum x1, blocking collectives, body(): sum_query, sum_square = lax.psum((sum_query, sum_square), 'seq')  31 us
    dot_general x1, matrix products, body(): jnp.einsum('hd,nd->hn', w_down, incoming, preferred_element_type=jnp.floa...  7.93 us
  transfers between devices with their start and end apart: 2, of which 2 were waited for; matrix products, arithmetic and copies ran while one was open for 2% of the time, Pallas kernels for 0%

commit v1 on v0

v1 whole, which is shorter than its diff:
```python
import functools
import math

import jax
import jax.numpy as jnp
from jax import lax
from jax.experimental import pallas as pl
from jax.experimental.pallas import tpu as pltpu
from jax.sharding import PartitionSpec as P

MESH = pl.DeviceIdType.MESH
F32 = jnp.float32
BF16 = jnp.bfloat16
EPSILON = 1e-06
NT = (((1,), (1,)), ((), ()))
NN = (((1,), (0,)), ((), ()))
TN = (((0,), (0,)), ((), ()))


def mm(a, b, dims):
    return lax.dot_general(a, b, dims, preferred_element_type=F32)


def column(row):
    n = row.shape[1]
    return jnp.transpose(jnp.broadcast_to(row, (n, n)))


def gelu_slope(pre_act):
    normal_cdf = 0.5 * (1.0 + lax.erf(pre_act * 0.7071067811865476))
    density = jnp.exp(-0.5 * pre_act * pre_act) * 0.3989422804014327
    return normal_cdf + pre_act * density


def kernel(
    model_width,
    vg_any, wv_any, gain_ref, pos_ref, own_ref, span_ref, vp_any, vr_any, qh_any, wd_any, pre_any,
    out_ref, ques_ref,
    vg, wv, vp, vr, qh, wd, pre,
    snd1, sc1, r1, rs1, snd2, sc2, r2, rs2,
    h, relay1, stage1, near1, g1, relay2, stage2, near2, place, slope, snd3, r3,
    load_sem, ex_send, ex_recv, red_send, red_recv, z_send, z_recv, z_near,
):
    s = lax.axis_index("seq")
    f = lax.axis_index("frame")
    y, x = s // 4, s % 4
    z, core = f // 2, f % 2

    barrier = pltpu.get_barrier_semaphore()

    def greet(k, carry):
        pl.semaphore_signal(barrier, inc=1, device_id=(lax.rem(s + k, 16), f), device_id_type=MESH)
        return carry

    lax.fori_loop(1, 16, greet, 0)

    def z_device(step, other):
        return ((z + step + 32) % 32) * 2 + (core + other) % 2

    for step, other in ((0, 1), (1, 0), (1, 1), (-1, 0), (-1, 1)):
        pl.semaphore_signal(barrier, inc=1, device_id=(s, z_device(step, other)), device_id_type=MESH)

    loads = [
        pltpu.make_async_copy(src, dst, load_sem.at[i])
        for i, (src, dst) in enumerate(
            ((vg_any.at[0], vg), (vp_any.at[0], vp), (qh_any.at[0], qh), (vr_any.at[0], vr), (wv_any, wv), (pre_any.at[0], pre), (wd_any, wd))
        )
    ]
    for load in loads:
        load.start()
    load_vg, load_vp, load_qh, load_vr, load_wv, load_pre, load_wd = loads

    shard_len = vg.shape[0]
    tokens = vp.shape[0]
    lanes = lax.broadcasted_iota(jnp.int32, (tokens, 128), 1)

    place_of = column(pos_ref[...].astype(F32) - (s * shard_len).astype(F32))
    lane_value = lanes.astype(F32)
    select = jnp.concatenate(
        [(place_of == lane_value + float(128 * i)).astype(F32).astype(BF16) for i in range(shard_len // 128)], axis=1
    )
    load_vg.wait()
    own_rows = mm(select, vg[...], NN)

    load_qh.wait()
    count = span_ref[:, 1:2].astype(F32)
    start = span_ref[:, 0:1]
    rows32 = lax.broadcasted_iota(jnp.int32, (qh.shape[0], 1), 0)
    span_mask = ((rows32 >= start) & (rows32 < start + span_ref[:, 1:2])).astype(F32)
    quest_mean = jnp.sum(span_mask * qh[...].astype(F32), axis=0, keepdims=True) / count
    load_vp.wait()
    projected = vp[...].astype(F32)
    gain = gain_ref[...]
    scaled = gain * projected
    scaled_hi = scaled.astype(BF16)
    scaled_lo = (scaled - scaled_hi.astype(F32)).astype(BF16)
    load_wv.wait()
    mixed = mm(scaled_hi, wv[...], NN) + mm(scaled_lo, wv[...], NN)
    sum_query = jnp.sum(projected * quest_mean, axis=1, keepdims=True)
    sum_square = jnp.sum(projected * projected, axis=1, keepdims=True)
    load_vr.wait()
    sum_resid = jnp.sum(vr[...].astype(F32) * projected, axis=1, keepdims=True)
    sums = jnp.where(lanes == 0, sum_query, jnp.where(lanes == 1, sum_square, jnp.where(lanes == 2, sum_resid, 0.0)))
    width = own_rows.shape[1]
    snd1[...] = jnp.concatenate([own_rows.reshape(16, 8, width), mixed.reshape(16, 8, width)], axis=1).astype(BF16)
    sc1[...] = sums.reshape(16, 8, 128)

    pl.semaphore_wait(barrier, 20)

    def send1(k, carry):
        t = lax.rem(s + k, 16)
        pltpu.make_async_remote_copy(
            src_ref=snd1.at[t], dst_ref=r1.at[s], send_sem=ex_send.at[0], recv_sem=ex_recv.at[0], device_id=(t, f), device_id_type=MESH
        ).start()
        pltpu.make_async_remote_copy(
            src_ref=sc1.at[t], dst_ref=rs1.at[s], send_sem=ex_send.at[1], recv_sem=ex_recv.at[1], device_id=(t, f), device_id_type=MESH
        ).start()
        return carry

    lax.fori_loop(1, 16, send1, 0)
    r1[pl.ds(s, 1)] = snd1[pl.ds(s, 1)]
    rs1[pl.ds(s, 1)] = sc1[pl.ds(s, 1)]

    def z_tell(level):
        for step in (1 << level, -(1 << level)):
            pl.semaphore_signal(z_near.at[level], inc=1, device_id=(s, z_device(step, 0)), device_id_type=MESH)

    z_tell(0)
    owner = own_ref[...]
    owner_value = owner.astype(F32)
    same = (column(owner_value) == owner_value) & (lax.broadcasted_iota(jnp.int32, (tokens, tokens), 0) < lanes)
    rank = jnp.sum(same.astype(F32), axis=0, keepdims=True)
    target = owner_value * 4.0 + rank
    rows = place.shape[0]
    target2 = jnp.concatenate([target, target], axis=1)
    row_id = lax.broadcasted_iota(jnp.int32, (rows, 1), 0)
    slot_of_row = ((row_id >> 3) * 4 + (row_id & 3)).astype(F32)
    half_of_row = (row_id >> 2) & 1
    lane_half = lax.broadcasted_iota(jnp.int32, (1, 2 * tokens), 1) >> 7
    place[...] = ((target2 == slot_of_row) & (half_of_row == lane_half)).astype(F32).astype(BF16)
    pl.semaphore_wait(z_near.at[0], 2)
    z_tell(1)
    load_pre.wait()
    slope[...] = gelu_slope(pre[...].astype(F32))
    pl.semaphore_wait(z_near.at[1], 2)
    z_tell(2)

    def wait_all(buffer, amount, sems, i):
        view = buffer.at[pl.ds(0, amount)]
        pltpu.make_async_copy(view, view, sems.at[i]).wait()

    wait_all(r1, 15, ex_recv, 0)
    wait_all(rs1, 15, ex_recv, 1)
    total = r1[0].astype(F32)
    sums = rs1[0]
    for i in range(1, 16):
        total = total + r1[i].astype(F32)
        sums = sums + rs1[i]
    picked8 = total[0:8]
    sum_norm = jnp.sum(picked8 * total[8:16], axis=1, keepdims=True)
    sum_query, sum_square, sum_resid = sums[:, 0:1], sums[:, 1:2], sums[:, 2:3]
    gate_scale = 4.0 / math.sqrt(model_width)
    gate = jax.nn.sigmoid(gate_scale * sum_query)
    inv_rms = lax.rsqrt(gate * gate * sum_square / model_width + EPSILON)
    coef = gate * inv_rms * inv_rms * inv_rms * (gate * sum_norm) / model_width
    gate_grad = sum_resid + inv_rms * sum_norm - coef * sum_square
    logit = gate_grad * gate * (1.0 - gate) * gate_scale
    lanes8 = lanes[0:8]
    sc2[...] = jnp.where(
        lanes8 == 0, gate, jnp.where(lanes8 == 1, inv_rms, jnp.where(lanes8 == 2, coef, jnp.where(lanes8 == 3, logit, 0.0)))
    )
    snd2[...] = picked8.astype(BF16)

    def send2(k, carry):
        t = lax.rem(s + k, 16)
        pltpu.make_async_remote_copy(
            src_ref=snd2, dst_ref=r2.at[s], send_sem=ex_send.at[2], recv_sem=ex_recv.at[2], device_id=(t, f), device_id_type=MESH
        ).start()
        pltpu.make_async_remote_copy(
            src_ref=sc2, dst_ref=rs2.at[s], send_sem=ex_send.at[3], recv_sem=ex_recv.at[3], device_id=(t, f), device_id_type=MESH
        ).start()
        return carry

    lax.fori_loop(1, 16, send2, 0)
    r2[pl.ds(s, 1)] = snd2[...][None]
    rs2[pl.ds(s, 1)] = sc2[...][None]
    pl.semaphore_wait(z_near.at[2], 2)
    z_tell(3)
    load_wd.wait()
    wait_all(r2, 15, ex_recv, 2)
    wait_all(rs2, 15, ex_recv, 3)

    picked = r2[...].astype(F32).reshape(tokens, width).astype(BF16)
    scalars = rs2[...].reshape(tokens, 128)
    normed_grad = mm(picked, wv[...], NT)
    projected = vp[...].astype(F32)
    logit_all = scalars[:, 3:4]
    input_grad = vr[...].astype(F32) + scalars[:, 1:2] * gain * normed_grad - scalars[:, 2:3] * projected
    proj_grad = (scalars[:, 0:1] * input_grad + logit_all * quest_mean).astype(BF16)

    def hop(half, second, step):
        if (half == 0) != second:
            return y * 4 + (x + step + 4) % 4, f
        return ((y + step + 4) % 4) * 4 + x, f

    def at(half, second, step):
        coord = x if (half == 0) != second else y
        return (coord + step + 4) % 4

    def products(half, c, step):
        major = at(half, False, step)
        blocks = []
        for minor in range(4):
            block = (minor * 4 + major) if half == 0 else (major * 4 + minor)
            blocks.append(wd[pl.ds(pl.multiple_of(block * 512 + half * 256 + c * 128, 128), 128), :])
        h[half, c, major] = mm(jnp.concatenate(blocks, axis=0), proj_grad, NT).astype(BF16)

    started = []

    def ship(src, dst, second, half, c, which, step):
        copy = pltpu.make_async_remote_copy(
            src_ref=src, dst_ref=dst, send_sem=red_send.at[int(second), half, c, which], recv_sem=red_recv.at[int(second), half, c, which],
            device_id=hop(half, second, step), device_id_type=MESH,
        )
        copy.start()
        started.append(copy)
        return copy

    copies = {}

    def first_sends(second, half, c):
        if second:
            size = 64
            part = lambda step, low: g1.at[half, c, pl.ds(at(half, True, step) * 128 + low * size, size)]
            relay, near = relay2, near2
        else:
            size = 256
            part = lambda step, low: h.at[half, c, at(half, False, step), pl.ds(low * size, size)]
            relay, near = relay1, near1
        copies[second, half, c, 0] = ship(part(2, 0), relay.at[half, c, 0], second, half, c, 0, 1)
        copies[second, half, c, 1] = ship(part(2, 1), relay.at[half, c, 1], second, half, c, 1, -1)
        copies[second, half, c, 2] = ship(part(1, 1), near.at[half, c, 0, pl.ds(size, size)], second, half, c, 2, 1)
        copies[second, half, c, 3] = ship(part(-1, 0), near.at[half, c, 1, pl.ds(0, size)], second, half, c, 3, -1)

    def second_sends(second, half, c):
        if second:
            size = 64
            own = lambda step, low: g1[half, c, pl.ds(at(half, True, step) * 128 + low * size, size)]
            relay, near, stage = relay2, near2, stage2
        else:
            size = 256
            own = lambda step, low: h[half, c, at(half, False, step), low * size:(low + 1) * size]
            relay, near, stage = relay1, near1, stage1
        for i, step in ((0, 1), (1, -1)):
            copies[second, half, c, i].wait_recv()
            stage[half, c, i] = (own(step, i).astype(F32) + relay[half, c, i].astype(F32)).astype(BF16)
            copies[second, half, c, 4 + i] = ship(
                stage.at[half, c, i], near.at[half, c, i, pl.ds(i * size, size)], second, half, c, 4 + i, step
            )

    def collect(second, half, c):
        for which in (2, 3, 4, 5):
            copies[second, half, c, which].wait_recv()
        if second:
            mine = g1[half, c, pl.ds(at(half, True, 0) * 128, 128)]
            return mine.astype(F32) + near2[half, c, 0].astype(F32) + near2[half, c, 1].astype(F32)
        mine = h[half, c, at(half, False, 0)]
        return mine.astype(F32) + near1[half, c, 0].astype(F32) + near1[half, c, 1].astype(F32)

    def z_target(k):
        far = jnp.where(k < 2, 16, 15 - (k - 2) // 4)
        sign = jnp.where(k < 2, 1, jnp.where(((k - 2) // 2) % 2 == 0, 1, -1))
        target = ((z + sign * far + 64) % 32) * 2 + (core + k) % 2
        return jnp.where(k == 62, z * 2 + (1 - core), target)

    def route(c):
        both = jnp.concatenate([collect(True, 0, c), collect(True, 1, c)], axis=1).astype(BF16)
        snd3[c] = mm(place[...], both, NT).reshape(64, 8, 128).astype(BF16)

        def send3(k, carry):
            t = z_target(k)
            pltpu.make_async_remote_copy(
                src_ref=snd3.at[c, t], dst_ref=r3.at[c, f], send_sem=z_send.at[c], recv_sem=z_recv.at[c], device_id=(s, t), device_id_type=MESH
            ).start()
            return carry

        lax.fori_loop(0, 63, send3, 0)
        r3[c, pl.ds(f, 1)] = snd3[c, pl.ds(f, 1)]

    halves = (0, 1)
    for half in halves:
        products(half, 0, 2)
    for half in halves:
        products(half, 0, 1)
        products(half, 0, -1)
        first_sends(False, half, 0)
    for half in halves:
        products(half, 0, 0)
        products(half, 1, 2)
        products(half, 1, 1)
        products(half, 1, -1)
    for half in halves:
        second_sends(False, half, 0)
        first_sends(False, half, 1)
    for half in halves:
        products(half, 1, 0)
    ques_row = jnp.sum(logit_all * projected, axis=0, keepdims=True)
    ques_ref[0] = (span_mask * ques_row / count).astype(BF16)
    for half in halves:
        g1[half, 0] = collect(False, half, 0).astype(BF16)
        first_sends(True, half, 0)
    for half in halves:
        second_sends(False, half, 1)
    for half in halves:
        second_sends(True, half, 0)
    pl.semaphore_wait(z_near.at[3], 2)
    route(0)
    for half in halves:
        g1[half, 1] = collect(False, half, 1).astype(BF16)
        first_sends(True, half, 1)
    for half in halves:
        second_sends(True, half, 1)
    route(1)

    slots = out_ref.shape[2]
    row_id = lax.broadcasted_iota(jnp.int32, (rows, slots), 0)
    slot_id = lax.broadcasted_iota(jnp.int32, (rows, slots), 1)
    meets = (row_id >> 3) * 4 + (row_id & 3) == slot_id
    takes = [(meets & (((row_id >> 2) & 1) == half)).astype(F32).astype(BF16) for half in halves]
    for c in range(2):
        view = r3.at[c, pl.ds(0, 63)]
        pltpu.make_async_copy(view, view, z_recv.at[c]).wait()
        arrived = r3[c].astype(F32).reshape(rows, 128).astype(BF16)
        for half in halves:
            at_rows = slice(half * 256 + c * 128, half * 256 + c * 128 + 128)
            out_ref[0, at_rows] = (mm(arrived, takes[half], TN) * slope[at_rows]).astype(BF16)

    for c in range(2):
        view = r3.at[c, pl.ds(0, 63)]
        pltpu.make_async_copy(view, view, z_send.at[c]).wait()
    for copy in started:
        copy.wait_send()
    wait_all(r1, 15, ex_send, 0)
    wait_all(rs1, 15, ex_send, 1)
    wait_all(r2, 15, ex_send, 2)
    wait_all(rs2, 15, ex_send, 3)


def solution(mesh):
    def body(value_grad, w_value, norm_gain, vis_pos, frame_owner, ques_span, vis_proj, vis_resid, ques_hidden, w_down, pre_owned):
        model_width = vis_proj.shape[2] * mesh.shape["seq"]
        in_vmem = pl.BlockSpec(memory_space=pltpu.VMEM)
        in_any = pl.BlockSpec(memory_space=pl.ANY)
        dma = pltpu.SemaphoreType.DMA
        return pl.pallas_call(
            functools.partial(kernel, model_width),
            out_shape=(
                jax.ShapeDtypeStruct(pre_owned.shape, BF16),
                jax.ShapeDtypeStruct(ques_hidden.shape, BF16),
            ),
            in_specs=[in_any, in_any, in_vmem, in_vmem, in_vmem, in_vmem, in_any, in_any, in_any, in_any, in_any],
            out_specs=(in_vmem, in_vmem),
            scratch_shapes=[
                pltpu.VMEM((1024, 512), BF16),
                pltpu.VMEM((512, 512), BF16),
                pltpu.VMEM((128, 512), BF16),
                pltpu.VMEM((128, 512), BF16),
                pltpu.VMEM((32, 512), BF16),
                pltpu.VMEM((8192, 512), BF16),
                pltpu.VMEM((512, 256), BF16),
                pltpu.VMEM((16, 16, 512), BF16),
                pltpu.VMEM((16, 8, 128), F32),
                pltpu.VMEM((16, 16, 512), BF16),
                pltpu.VMEM((16, 8, 128), F32),
                pltpu.VMEM((8, 512), BF16),
                pltpu.VMEM((8, 128), F32),
                pltpu.VMEM((16, 8, 512), BF16),
                pltpu.VMEM((16, 8, 128), F32),
                pltpu.VMEM((2, 2, 4, 512, 128), BF16),
                pltpu.VMEM((2, 2, 2, 256, 128), BF16),
                pltpu.VMEM((2, 2, 2, 256, 128), BF16),
                pltpu.VMEM((2, 2, 2, 512, 128), BF16),
                pltpu.VMEM((2, 2, 512, 128), BF16),
                pltpu.VMEM((2, 2, 2, 64, 128), BF16),
                pltpu.VMEM((2, 2, 2, 64, 128), BF16),
                pltpu.VMEM((2, 2, 2, 128, 128), BF16),
                pltpu.VMEM((512, 256), BF16),
                pltpu.VMEM((512, 256), F32),
                pltpu.VMEM((2, 64, 8, 128), BF16),
                pltpu.VMEM((2, 64, 8, 128), BF16),
                dma((7,)),
                dma((4,)),
                dma((4,)),
                dma((2, 2, 2, 6)),
                dma((2, 2, 2, 6)),
                dma((2,)),
                dma((2,)),
                pltpu.SemaphoreType.REGULAR((4,)),
            ],
            compiler_params=pltpu.CompilerParams(collective_id=0, has_side_effects=True, vmem_limit_bytes=56 * 1024 * 1024),
        )(
            value_grad,
            w_value,
            norm_gain.reshape(1, -1),
            vis_pos,
            frame_owner.reshape(1, -1),
            ques_span,
            vis_proj,
            vis_resid,
            ques_hidden,
            w_down,
            pre_owned,
        )

    in_specs = (
        P("frame", "seq", None),
        P("seq", None),
        P("seq"),
        P("frame", None),
        P("frame", None, None),
        P("frame", None),
        P("frame", None, "seq"),
        P("frame", None, "seq"),
        P("frame", None, "seq"),
        P(None, "seq"),
        P("frame", "seq", None),
    )
    out_specs = (P("frame", "seq", None), P("frame", None, "seq"))
    return jax.shard_map(body, mesh=mesh, in_specs=in_specs, out_specs=out_specs, check_vma=False)
```

time: 390 us -> 81.1 us (0.21)
  waiting for transfers between devices: 245 us -> 0 us
  blocking collectives: 105 us -> 0 us
  Pallas kernels: 0 us -> 77.2 us
  between operations: 16 us -> 0.64 us
  matrix products: 13.4 us -> 0 us
  other arithmetic: 5.01 us -> 0 us
    psum x1 -> x0, waiting for transfers between devices: 156 us -> none  [body(): picked = lax.psum(own_rows.astype(jnp.bfloat16), 'seq')]
    reduce_scatter x1 -> x0, waiting for transfers between devices: 89.3 us -> none  [body(): lax.psum_scatter(jnp.einsum('hd,nd->hn', w_down, incoming, preferred_elem...]
    pallas_call x0 -> x1, Pallas kernels: none -> 77.2 us  [body(): pl.pallas_call(functools.partial(kernel, model_width), out_shape=(jax.Sha...]
    all_to_all x1 -> x0, blocking collectives: 73.8 us -> none  [body(): lax.all_to_all(outgoing, 'frame', split_axis=0, concat_axis=0, tiled=True)]
    psum x1 -> x0, blocking collectives: 31 us -> none  [body(): sum_query, sum_square = lax.psum((sum_query, sum_square), 'seq')]
    dot_general x5 -> x0, matrix products: 13.4 us -> none  [the longest x1 7.93 us: body(): jnp.einsum('hd,nd->hn', w_down, incoming, preferred_element_type=jnp.floa...]
  transfers between devices with their start and end apart: 2 -> 0, of which waited for: 2 -> 0; matrix products, arithmetic and copies ran while one was open for 2% -> 0% of each run, Pallas kernels for 0% -> 0%
where the time goes in v1:
time: 81.1 us; the launch traced here: 80.8 us
  Pallas kernels  77.2 us (95%)
  local copies, waits for them, and re-layouts  3.04 us (4%)
    pallas_call x1, Pallas kernels, body(): pl.pallas_call(functools.partial(kernel, model_width), out_shape=(jax.Sha...  77.2 us
    unnamed x2, local copies, waits for them, and re-layouts  3.04 us

profile of v1, /device:TPU:1, one launch (start us, length us, event | category | flops | bytes accessed | tf_op | source)
XLA Modules:
  0.0 80.8 jit_solution(16375731578945510234)
XLA Ops:
  0.6 77.2 %shard_map.122 = (bf16[1,512,256]{2,1,0:T(8,128)(2,1)}, bf16[1,32,512]{2,1,0:T(8,128)(2,1)}) custom-call(bf16[1,1024,512]{2,1,0:T(8,128)(2,1)} %vg_any.1, bf16[512,512]{1,0:T(8,128)(2,1)} %wv_any.1, f32[1,512]{1,0:T(1,128)} %bitcast.2, s32[1,128]{1,0:T(1,128)} %pos_ref.1, s32[1,128]{1,0:T(1,128)} %bitcast.3, s32[1,2]{1,0:T(1,128)} %span_ref.1, ...), custom_call_target="tpu_custom_call" | custom-call | tf_op jit(solution)/shard_map/pallas_call | solution.py:355
  77.8 1.7 %copy.15 = bf16[1,512,256]{2,1,0:T(8,128)(2,1)} copy(bf16[1,512,256]{2,1,0:T(8,128)(2,1)} %get-tuple-element.4) | data formatting | bytes 524288
  79.5 1.4 %copy.16 = bf16[1,32,512]{2,1,0:T(8,128)(2,1)} copy(bf16[1,32,512]{2,1,0:T(8,128)(2,1)} %get-tuple-element.5) | data formatting | bytes 65536

commit v2 on v1

v2 whole, which is shorter than its diff:
```python
import functools
import math

import jax
import jax.numpy as jnp
from jax import lax
from jax.experimental import pallas as pl
from jax.experimental.pallas import tpu as pltpu
from jax.sharding import PartitionSpec as P

MESH = pl.DeviceIdType.MESH
F32 = jnp.float32
BF16 = jnp.bfloat16
EPSILON = 1e-06
NT = (((1,), (1,)), ((), ()))
NN = (((1,), (0,)), ((), ()))
TN = (((0,), (0,)), ((), ()))


def mm(a, b, dims):
    return lax.dot_general(a, b, dims, preferred_element_type=F32)


def column(row):
    n = row.shape[1]
    return jnp.transpose(jnp.broadcast_to(row, (n, n)))


def triple(values):
    high = values.astype(BF16).astype(F32)
    rest = values - high
    middle = rest.astype(BF16).astype(F32)
    low = (rest - middle).astype(BF16).astype(F32)
    return high + pltpu.roll(middle, 8, 1) + pltpu.roll(low, 16, 1)


def untriple(terms):
    return terms[:, 0:8] + terms[:, 8:16] + terms[:, 16:24]


def gelu_slope(pre_act):
    normal_cdf = 0.5 * (1.0 + lax.erf(pre_act * 0.7071067811865476))
    density = jnp.exp(-0.5 * pre_act * pre_act) * 0.3989422804014327
    return normal_cdf + pre_act * density


def kernel(
    model_width,
    vg_any, wv_any, gain_any, pos_any, own_any, span_any, vp_any, vr_any, qh_any, wd_any, pre_any,
    out_ref, ques_ref,
    vg, wv, gain_ref, pos_ref, own_ref, span_ref, vp, vr, qh, wd, pre,
    snd1, r1, snd2, r2,
    h, relay1, stage1, near1, g1, near2, place, slope, snd3, r3,
    load_sem, ex_send, ex_recv, red_send, red_recv, z_send, z_recv, z_near,
):
    s = lax.axis_index("seq")
    f = lax.axis_index("frame")
    y, x = s // 4, s % 4
    z, core = f // 2, f % 2

    ys = [y] + [(y + step) % 4 for step in (1, 2, 3)]
    xs = [x] + [(x + step) % 4 for step in (1, 2, 3)]
    hops = (0, 1, 2, 1)
    offsets = sorted(((i, j) for i in range(4) for j in range(4) if i or j), key=lambda o: -hops[o[0]] - hops[o[1]])
    others = [ys[i] * 4 + xs[j] for i, j in offsets]

    copies_in = [
        pltpu.make_async_copy(src, dst, load_sem.at[i])
        for i, (src, dst) in enumerate(
            (
                (pos_any, pos_ref), (vg_any.at[0], vg), (qh_any.at[0], qh), (span_any, span_ref), (vp_any.at[0], vp), (gain_any, gain_ref),
                (wv_any, wv), (vr_any.at[0], vr), (own_any, own_ref), (pre_any.at[0], pre), (wd_any, wd),
            )
        )
    ]
    load_pos, load_vg, load_qh, load_span, load_vp, load_gain, load_wv, load_vr, load_own, load_pre, load_wd = copies_in
    load_pos.start()
    load_vg.start()

    barrier = pltpu.get_barrier_semaphore()
    for t in others:
        pl.semaphore_signal(barrier, inc=1, device_id=(t, f), device_id_type=MESH)

    def z_device(step, other):
        return ((z + step + 32) % 32) * 2 + (core + other) % 2

    for step, other in ((1, 0), (1, 1), (-1, 0), (-1, 1), (0, 1)):
        pl.semaphore_signal(barrier, inc=1, device_id=(s, z_device(step, other)), device_id_type=MESH)
    for load in copies_in[2:]:
        load.start()

    shard_len = vg.shape[0]
    tokens = vp.shape[0]
    lanes = lax.broadcasted_iota(jnp.int32, (tokens, 128), 1)

    load_pos.wait()
    place_of = column(pos_ref[...].astype(F32) - (s * shard_len).astype(F32))
    lane_value = lanes.astype(F32)
    select = jnp.concatenate(
        [(place_of == lane_value + float(128 * i)).astype(F32).astype(BF16) for i in range(shard_len // 128)], axis=1
    )
    load_vg.wait()
    own_rows = mm(select, vg[...], NN)

    load_qh.wait()
    load_span.wait()
    count = span_ref[:, 1:2].astype(F32)
    start = span_ref[:, 0:1]
    rows32 = lax.broadcasted_iota(jnp.int32, (qh.shape[0], 1), 0)
    span_mask = ((rows32 >= start) & (rows32 < start + span_ref[:, 1:2])).astype(F32)
    quest_mean = jnp.sum(span_mask * qh[...].astype(F32), axis=0, keepdims=True) / count
    load_vp.wait()
    projected = vp[...].astype(F32)
    load_gain.wait()
    gain = gain_ref[...]
    scaled = gain * projected
    scaled_hi = scaled.astype(BF16)
    scaled_lo = (scaled - scaled_hi.astype(F32)).astype(BF16)
    load_wv.wait()
    mixed = mm(scaled_hi, wv[...], NN) + mm(scaled_lo, wv[...], NN)
    sum_query = jnp.sum(projected * quest_mean, axis=1, keepdims=True)
    sum_square = jnp.sum(projected * projected, axis=1, keepdims=True)
    load_vr.wait()
    sum_resid = jnp.sum(vr[...].astype(F32) * projected, axis=1, keepdims=True)
    sums = jnp.where(lanes == 0, sum_query, jnp.where(lanes == 1, sum_square, jnp.where(lanes == 2, sum_resid, 0.0)))
    width = own_rows.shape[1]
    for at_rows, part in ((slice(0, 8), own_rows), (slice(8, 16), mixed)):
        snd1[:, at_rows, 0:width] = part.reshape(16, 8, width).astype(BF16)
    snd1[:, 0:8, width:] = triple(sums).reshape(16, 8, 128).astype(BF16)
    snd1[:, 8:16, width:] = jnp.zeros((16, 8, 128), BF16)

    pl.semaphore_wait(barrier, 20)

    def exchange(source, buffer, i):
        for t in others:
            pltpu.make_async_remote_copy(
                src_ref=source(t), dst_ref=buffer.at[s], send_sem=ex_send.at[i], recv_sem=ex_recv.at[i], device_id=(t, f), device_id_type=MESH
            ).start()

    exchange(lambda t: snd1.at[t], r1, 0)
    r1[pl.ds(s, 1)] = snd1[pl.ds(s, 1)]

    def z_tell(level):
        for step in (1 << level, -(1 << level)):
            pl.semaphore_signal(z_near.at[level], inc=1, device_id=(s, z_device(step, 0)), device_id_type=MESH)

    z_tell(0)
    load_own.wait()
    owner = own_ref[...]
    owner_value = owner.astype(F32)
    same = (column(owner_value) == owner_value) & (lax.broadcasted_iota(jnp.int32, (tokens, tokens), 0) < lanes)
    rank = jnp.sum(same.astype(F32), axis=0, keepdims=True)
    target = owner_value * 4.0 + rank
    rows = place.shape[0]
    target2 = jnp.concatenate([target, target], axis=1)
    row_id = lax.broadcasted_iota(jnp.int32, (rows, 1), 0)
    slot_of_row = ((row_id >> 3) * 4 + (row_id & 3)).astype(F32)
    half_of_row = (row_id >> 2) & 1
    lane_half = lax.broadcasted_iota(jnp.int32, (1, 2 * tokens), 1) >> 7
    place[...] = ((target2 == slot_of_row) & (half_of_row == lane_half)).astype(F32).astype(BF16)
    pl.semaphore_wait(z_near.at[0], 2)
    z_tell(1)
    load_pre.wait()
    slope[...] = gelu_slope(pre[...].astype(F32))
    pl.semaphore_wait(z_near.at[1], 2)
    z_tell(2)

    def wait_all(buffer, amount, sems, i):
        view = buffer.at[pl.ds(0, amount)]
        pltpu.make_async_copy(view, view, sems.at[i]).wait()

    wait_all(r1, 15, ex_recv, 0)
    total = r1[0].astype(F32)
    for i in range(1, 16):
        total = total + r1[i].astype(F32)
    picked8 = total[0:8, 0:width]
    sum_norm = jnp.sum(picked8 * total[8:16, 0:width], axis=1, keepdims=True)
    sums = untriple(total[0:8, width:])
    sum_query, sum_square, sum_resid = sums[:, 0:1], sums[:, 1:2], sums[:, 2:3]
    gate_scale = 4.0 / math.sqrt(model_width)
    gate = jax.nn.sigmoid(gate_scale * sum_query)
    inv_rms = lax.rsqrt(gate * gate * sum_square / model_width + EPSILON)
    coef = gate * inv_rms * inv_rms * inv_rms * (gate * sum_norm) / model_width
    gate_grad = sum_resid + inv_rms * sum_norm - coef * sum_square
    logit = gate_grad * gate * (1.0 - gate) * gate_scale
    lanes8 = lanes[0:8]
    scalars = jnp.where(
        lanes8 == 0, gate, jnp.where(lanes8 == 1, inv_rms, jnp.where(lanes8 == 2, coef, jnp.where(lanes8 == 3, logit, 0.0)))
    )
    snd2[:, 0:width] = picked8.astype(BF16)
    snd2[:, width:] = triple(scalars).astype(BF16)
    exchange(lambda t: snd2, r2, 1)
    r2[pl.ds(s, 1)] = snd2[...][None]
    pl.semaphore_wait(z_near.at[2], 2)
    z_tell(3)
    load_wd.wait()
    wait_all(r2, 15, ex_recv, 1)

    gathered = r2[...].astype(F32).reshape(tokens, width + 128)
    picked = gathered[:, 0:width].astype(BF16)
    scalars = untriple(gathered[:, width:])
    normed_grad = mm(picked, wv[...], NT)
    projected = vp[...].astype(F32)
    logit_all = scalars[:, 3:4]
    input_grad = vr[...].astype(F32) + scalars[:, 1:2] * gain * normed_grad - scalars[:, 2:3] * projected
    proj_grad = (scalars[:, 0:1] * input_grad + logit_all * quest_mean).astype(BF16)

    def hop(half, second, step):
        if (half == 0) != second:
            return y * 4 + (x + step + 4) % 4, f
        return ((y + step + 4) % 4) * 4 + x, f

    def at(half, second, step):
        coord = x if (half == 0) != second else y
        return (coord + step + 4) % 4

    def products(half, c, step):
        major = at(half, False, step)
        blocks = []
        for minor in range(4):
            block = (minor * 4 + major) if half == 0 else (major * 4 + minor)
            blocks.append(wd[pl.ds(pl.multiple_of(block * 512 + half * 256 + c * 128, 128), 128), :])
        h[half, c, major] = mm(jnp.concatenate(blocks, axis=0), proj_grad, NT).astype(BF16)

    def ship(src, dst, second, half, c, which, step):
        copy = pltpu.make_async_remote_copy(
            src_ref=src, dst_ref=dst, send_sem=red_send.at[int(second)], recv_sem=red_recv.at[half, c, which],
            device_id=hop(half, second, step), device_id_type=MESH,
        )
        copy.start()
        return copy

    copies = {}

    def first_sends(half, c, whiches):
        def part(step, low):
            return h.at[half, c, at(half, False, step), pl.ds(low * 256, 256)]

        plan = (
            (part(2, 0), relay1.at[half, c, 0], 1),
            (part(2, 1), relay1.at[half, c, 1], -1),
            (part(1, 1), near1.at[half, c, 0, pl.ds(256, 256)], 1),
            (part(-1, 0), near1.at[half, c, 1, pl.ds(0, 256)], -1),
        )
        for which in whiches:
            src, dst, way = plan[which]
            copies[half, c, which] = ship(src, dst, False, half, c, which, way)

    def relayed_sends(half, c):
        for i, step in ((0, 1), (1, -1)):
            copies[half, c, i].wait_recv()
            own = h[half, c, at(half, False, step), i * 256:(i + 1) * 256]
            stage1[half, c, i] = (own.astype(F32) + relay1[half, c, i].astype(F32)).astype(BF16)
            copies[half, c, 4 + i] = ship(
                stage1.at[half, c, i], near1.at[half, c, i, pl.ds(i * 256, 256)], False, half, c, 4 + i, step
            )

    def across(half, c):
        for which in (2, 3, 4, 5):
            copies[half, c, which].wait_recv()
        mine = h[half, c, at(half, False, 0)]
        g1[half, c] = (mine.astype(F32) + near1[half, c, 0].astype(F32) + near1[half, c, 1].astype(F32)).astype(BF16)
        for i, step in ((2, 2), (0, 1), (1, -1)):
            part = g1.at[half, c, pl.ds(pl.multiple_of(at(half, True, step) * 128, 128), 128)]
            copies[half, c, 6 + i] = ship(part, near2.at[half, c, i], True, half, c, 6 + i, step)

    def collect(half, c):
        total = g1[half, c, pl.ds(pl.multiple_of(at(half, True, 0) * 128, 128), 128)].astype(F32)
        for i in range(3):
            copies[half, c, 6 + i].wait_recv()
            total = total + near2[half, c, i].astype(F32)
        return total

    def z_target(k):
        far = jnp.where(k < 2, 16, 15 - (k - 2) // 4)
        sign = jnp.where(k < 2, 1, jnp.where(((k - 2) // 2) % 2 == 0, 1, -1))
        target = ((z + sign * far + 64) % 32) * 2 + (core + k) % 2
        return jnp.where(k == 62, z * 2 + (1 - core), target)

    def route(c, between=lambda: None):
        both = jnp.concatenate([collect(0, c), collect(1, c)], axis=1).astype(BF16)
        between()
        snd3[c] = mm(place[...], both, NT).reshape(64, 8, 128).astype(BF16)

        def send3(k, carry):
            t = z_target(k)
            pltpu.make_async_remote_copy(
                src_ref=snd3.at[c, t], dst_ref=r3.at[c, f], send_sem=z_send.at[c], recv_sem=z_recv.at[c], device_id=(s, t), device_id_type=MESH
            ).start()
            return carry

        lax.fori_loop(0, 63, send3, 0)
        r3[c, pl.ds(f, 1)] = snd3[c, pl.ds(f, 1)]

    halves = (0, 1)
    for half in halves:
        products(half, 0, 2)
        first_sends(half, 0, (0, 1))
    for half in halves:
        products(half, 0, 1)
        products(half, 0, -1)
        first_sends(half, 0, (2, 3))
    for half in halves:
        products(half, 0, 0)
        products(half, 1, 2)
        products(half, 1, 1)
        products(half, 1, -1)
    for half in halves:
        relayed_sends(half, 0)
    for half in halves:
        products(half, 1, 0)
    ques_row = jnp.sum(logit_all * projected, axis=0, keepdims=True)
    ques_ref[0] = (span_mask * ques_row / count).astype(BF16)

    def next_sends(whiches):
        for half in halves:
            first_sends(half, 1, whiches)

    for half in halves:
        across(half, 0)
    next_sends((0, 1))
    pl.semaphore_wait(z_near.at[3], 2)
    route(0, lambda: next_sends((2, 3)))
    for half in halves:
        relayed_sends(half, 1)
    for half in halves:
        across(half, 1)
    route(1)

    slots = out_ref.shape[2]
    row_id = lax.broadcasted_iota(jnp.int32, (rows, slots), 0)
    slot_id = lax.broadcasted_iota(jnp.int32, (rows, slots), 1)
    meets = (row_id >> 3) * 4 + (row_id & 3) == slot_id
    takes = [(meets & (((row_id >> 2) & 1) == half)).astype(F32).astype(BF16) for half in halves]
    for i, view in ((0, h.at[:, :, pl.ds(0, 3)]), (1, near2)):
        pltpu.make_async_copy(view, view, red_send.at[i]).wait()
    wait_all(r1, 15, ex_send, 0)
    wait_all(r2, 15, ex_send, 1)

    def wait_z(amount, c, sems):
        view = r3.at[c, pl.ds(0, amount)]
        pltpu.make_async_copy(view, view, sems.at[c]).wait()

    def finish(c):
        wait_z(63, c, z_recv)
        arrived = r3[c].astype(F32).reshape(rows, 128).astype(BF16)
        for half in halves:
            at_rows = slice(half * 256 + c * 128, half * 256 + c * 128 + 128)
            out_ref[0, at_rows] = (mm(arrived, takes[half], TN) * slope[at_rows]).astype(BF16)

    finish(0)
    for c in range(2):
        wait_z(63, c, z_send)
    finish(1)


def solution(mesh):
    def body(value_grad, w_value, norm_gain, vis_pos, frame_owner, ques_span, vis_proj, vis_resid, ques_hidden, w_down, pre_owned):
        model_width = vis_proj.shape[2] * mesh.shape["seq"]
        in_vmem = pl.BlockSpec(memory_space=pltpu.VMEM)
        in_hbm = pl.BlockSpec(memory_space=pltpu.HBM)
        dma = pltpu.SemaphoreType.DMA
        return pl.pallas_call(
            functools.partial(kernel, model_width),
            out_shape=(
                jax.ShapeDtypeStruct(pre_owned.shape, BF16),
                jax.ShapeDtypeStruct(ques_hidden.shape, BF16),
            ),
            in_specs=[in_hbm] * 11,
            out_specs=(in_vmem, in_vmem),
            scratch_shapes=[
                pltpu.VMEM((1024, 512), BF16),
                pltpu.VMEM((512, 512), BF16),
                pltpu.VMEM((1, 512), F32),
                pltpu.VMEM((1, 128), jnp.int32),
                pltpu.VMEM((1, 128), jnp.int32),
                pltpu.VMEM((1, 2), jnp.int32),
                pltpu.VMEM((128, 512), BF16),
                pltpu.VMEM((128, 512), BF16),
                pltpu.VMEM((32, 512), BF16),
                pltpu.VMEM((8192, 512), BF16),
                pltpu.VMEM((512, 256), BF16),
                pltpu.VMEM((16, 16, 640), BF16),
                pltpu.VMEM((16, 16, 640), BF16),
                pltpu.VMEM((8, 640), BF16),
                pltpu.VMEM((16, 8, 640), BF16),
                pltpu.VMEM((2, 2, 4, 512, 128), BF16),
                pltpu.VMEM((2, 2, 2, 256, 128), BF16),
                pltpu.VMEM((2, 2, 2, 256, 128), BF16),
                pltpu.VMEM((2, 2, 2, 512, 128), BF16),
                pltpu.VMEM((2, 2, 512, 128), BF16),
                pltpu.VMEM((2, 2, 3, 128, 128), BF16),
                pltpu.VMEM((512, 256), BF16),
                pltpu.VMEM((512, 256), F32),
                pltpu.VMEM((2, 64, 8, 128), BF16),
                pltpu.VMEM((2, 64, 8, 128), BF16),
                dma((11,)),
                dma((2,)),
                dma((2,)),
                dma((2,)),
                dma((2, 2, 9)),
                dma((2,)),
                dma((2,)),
                pltpu.SemaphoreType.REGULAR((4,)),
            ],
            compiler_params=pltpu.CompilerParams(collective_id=0, has_side_effects=True, vmem_limit_bytes=24 * 1024 * 1024),
        )(
            *(
                pltpu.with_memory_space_constraint(value, pltpu.HBM)
                for value in (
                    value_grad,
                    w_value,
                    norm_gain.reshape(1, -1),
                    vis_pos,
                    frame_owner.reshape(1, -1),
                    ques_span,
                    vis_proj,
                    vis_resid,
                    ques_hidden,
                    w_down,
                    pre_owned,
                )
            )
        )

    in_specs = (
        P("frame", "seq", None),
        P("seq", None),
        P("seq"),
        P("frame", None),
        P("frame", None, None),
        P("frame", None),
        P("frame", None, "seq"),
        P("frame", None, "seq"),
        P("frame", None, "seq"),
        P(None, "seq"),
        P("frame", "seq", None),
    )
    out_specs = (P("frame", "seq", None), P("frame", None, "seq"))
    return jax.shard_map(body, mesh=mesh, in_specs=in_specs, out_specs=out_specs, check_vma=False)
```

time: 81.1 us -> 75.8 us (0.935)
  Pallas kernels: 77.2 us -> 73.7 us
  local copies, waits for them, and re-layouts: 3.04 us -> 1.32 us
    pallas_call x1, Pallas kernels: 77.2 us -> 73.7 us  [body(): pl.pallas_call(functools.partial(kernel, model_width), out_shape=(jax.Sha...]
    unnamed x2, local copies, waits for them, and re-layouts: 3.04 us -> 1.32 us
where the time goes in v2:
time: 75.8 us; the launch traced here: 75.7 us
  Pallas kernels  73.7 us (97%)
  local copies, waits for them, and re-layouts  1.32 us (2%)
    pallas_call x1, Pallas kernels, body(): pl.pallas_call(functools.partial(kernel, model_width), out_shape=(jax.Sha...  73.7 us

profile of v2, /device:TPU:1, one launch (start us, length us, event | category | flops | bytes accessed | tf_op | source)
XLA Modules:
  0.0 75.7 jit_solution(9351268136882671848)
XLA Ops:
  0.6 73.7 %shard_map.122 = (bf16[1,512,256]{2,1,0:T(8,128)(2,1)S(1)}, bf16[1,32,512]{2,1,0:T(8,128)(2,1)S(1)}) custom-call(bf16[1,1024,512]{2,1,0:T(8,128)(2,1)} %vg_any.1, bf16[512,512]{1,0:T(8,128)(2,1)} %wv_any.1, f32[1,512]{1,0:T(1,128)} %bitcast.2, s32[1,128]{1,0:T(1,128)} %pos_any.1, s32[1,128]{1,0:T(1,128)} %bitcast.3, s32[1,2]{1,0:T(1,128)} %span_any.1, ...), custom_call_target="tpu_custom_call" | custom-call | tf_op jit(solution)/shard_map/pallas_call | solution.py:363
  74.4 0.7 copy.15
  75.1 0.6 copy.16
